TPU v7x, 32 devices: a whole 2x2x4 slice. The times are simulated.
32 devices in a mesh: seq: 4 (over z), mp: 8 (over y, x, core).
Axes of the slice: x: 2, y: 2, z: 4, core: 2. Of those that a mesh axis runs over, the one named last changes fastest.
Arguments:
- ids: int32 [16, 1024], P('seq'), may hold values from 0 to 274
- lengths: int32 [1024], replicated, may hold values from 1 to 16, 12288 in all
- order: int32 [1024], replicated, may hold values from 0 to 1023, each once
- h_init: bfloat16 [2, 1024, 2048], P(None, 'seq', 'mp'), may hold values from -3 to 3
- c_init: float32 [2, 1024, 2048], P(None, 'seq', 'mp'), may hold values from -5 to 5
- embed: bfloat16 [2, 275, 100], replicated, may hold values from -5 to 5
- w_in: bfloat16 [2, 100, 8192], P(None, None, 'mp'), may hold values from -0.625 to 0.625
- w_rec: bfloat16 [2, 2048, 8192], P(None, None, 'mp'), may hold values from -0.125 to 0.125
- bias: float32 [2, 8192], P(None, 'mp'), may hold values from -3 to 3
- w_dec: bfloat16 [2, 2048, 275], P(None, 'mp'), may hold values from -0.75 to 0.75
- b_dec: float32 [2, 275], replicated, may hold values from -3 to 3
Outputs:
- loss: float32 [], replicated
- h_init_grad: float32 [2, 1024, 2048], P(None, 'seq', 'mp')
- c_init_grad: float32 [2, 1024, 2048], P(None, 'seq', 'mp')
- embed_grad: float32 [2, 275, 100], replicated
- w_in_grad: float32 [2, 100, 8192], P(None, None, ('mp', 'seq'))
- w_rec_grad: float32 [2, 2048, 8192], P(None, 'seq', 'mp')
- bias_grad: float32 [2, 8192], P(None, ('mp', 'seq'))
- w_dec_grad: float32 [2, 2048, 275], P(None, ('mp', 'seq'))
- b_dec_grad: float32 [2, 275], replicated
- rms_embed: float32 [2], replicated
- rms_hidden: float32 [2], replicated
- rms_logits: float32 [2], replicated
Inputs may be any that keep to these rules, and one draw needn't show every extreme that they name: `lengths`: they add up to 12288, and the longest stream is valid over all 16 positions. `order`: every stream stands in exactly one slot.
All inputs are finite; a program needn't handle non-finite values.
Results may differ from a plain program's by a relative error of at most 0.018.
Values may be sent and summed in bfloat16 or wider, within the bound.
A program may use at most 256 MiB of HBM per device.

v0:
```python
import jax
import jax.numpy as jnp
from jax import lax
from jax.sharding import PartitionSpec as P


def column_order(own_units):
    lanes = min(128, own_units)
    source = jnp.arange(4 * lanes, dtype=jnp.int32)
    place = source % 4 * lanes + source // 4
    matrix = (place[:, None] == jnp.arange(4 * lanes, dtype=jnp.int32)[None, :]).astype(
        jnp.bfloat16
    )
    return (lanes, matrix)


def grouped(x, matrix):
    width = matrix.shape[0]
    parts = x.reshape(x.shape[:-1] + (x.shape[-1] // width, width))
    out = jnp.einsum("...gc,cp->...gp", parts, matrix, preferred_element_type=jnp.float32)
    return out.astype(x.dtype).reshape(x.shape)


def ungrouped(x, matrix):
    return grouped(x, matrix.T)


def ungrouped_wide(x, lanes):
    parts = x.reshape(x.shape[:-1] + (x.shape[-1] // (4 * lanes), 4, lanes))
    return jnp.swapaxes(parts, -1, -2).reshape(x.shape)


def gates_of(pre, lanes):
    parts = pre.reshape(pre.shape[:-1] + (pre.shape[-1] // (4 * lanes), 4, lanes))
    flat = pre.shape[:-1] + (pre.shape[-1] // 4,)
    return tuple((parts[..., k, :].reshape(flat) for k in range(4)))


def joined_gates(gates, lanes):
    split = [g.reshape(g.shape[:-1] + (g.shape[-1] // lanes, 1, lanes)) for g in gates]
    joined = jnp.concatenate(split, axis=-2)
    return joined.reshape(gates[0].shape[:-1] + (4 * gates[0].shape[-1],))


def recurrences(
    step_ids, own_len, h_init, c_init, embed, w_in, w_rec, bias, w_dec, wd_full, b_dec, count, lanes
):
    length, per_dev = step_ids.shape[1:]
    letter_count = embed.shape[1]
    steps = jnp.arange(length, dtype=jnp.int32)
    live_steps = jnp.stack(
        [steps[:, None] < own_len[None, :], (length - 1 - steps)[:, None] < own_len[None, :]],
        axis=1,
    )[..., None]
    letters = jnp.arange(letter_count, dtype=jnp.int32)
    onehot = (jnp.swapaxes(step_ids, 0, 1)[..., None] == letters).astype(jnp.bfloat16)
    letter_rows = jnp.einsum(
        "sdbv,dve->sdbe", onehot, embed, preferred_element_type=jnp.float32
    ).astype(jnp.bfloat16)
    gates_in = jnp.einsum(
        "sdbe,dec->sdbc", letter_rows, w_in, preferred_element_type=jnp.float32
    ).astype(jnp.bfloat16)

    def forward_step(carry, inputs):
        hidden, cell = carry
        gate_in, live = inputs
        whole = lax.all_gather(hidden, "mp", axis=2, tiled=True)
        recurrent = jnp.einsum("dbh,dhc->dbc", whole, w_rec, preferred_element_type=jnp.float32)
        pre = gate_in.astype(jnp.float32) + recurrent + bias[:, None]
        in_pre, forget_pre, cell_pre, out_pre = gates_of(pre, lanes)
        in_gate, forget, out_gate = (jax.nn.sigmoid(x) for x in (in_pre, forget_pre, out_pre))
        cell_gate = jnp.tanh(cell_pre)
        new_cell = forget * cell + in_gate * cell_gate
        cell_next = jnp.where(live, new_cell, cell)
        hidden_next = jnp.where(
            live, out_gate * jnp.tanh(new_cell), hidden.astype(jnp.float32)
        ).astype(jnp.bfloat16)
        return ((hidden_next, cell_next), (whole, cell, in_gate, forget, cell_gate, out_gate))

    (last_hidden, last_cell), (wholes, cells, *gates) = lax.scan(
        forward_step, (h_init, c_init), (gates_in, live_steps)
    )
    last_whole = lax.all_gather(last_hidden, "mp", axis=2, tiled=True)
    after = jnp.concatenate([wholes[1:], last_whole[None]], axis=0)
    own = h_init.shape[2]
    mine = lax.dynamic_slice_in_dim(after, lax.axis_index("mp") * own, own, axis=3)
    mine_wide = mine.astype(jnp.float32)
    hidden_sq = jnp.sum(jnp.where(live_steps, mine_wide * mine_wide, 0.0), axis=(0, 2, 3))
    logits = (
        jnp.einsum("sdbh,dhv->sdbv", after, wd_full, preferred_element_type=jnp.float32)
        + b_dec[None, :, None]
    )
    targets = jnp.swapaxes(jnp.concatenate([step_ids[:, 1:], step_ids[:, :1]], axis=1), 0, 1)
    fore_valid = steps[:, None] + 1 < own_len[None, :]
    back_valid = (steps[:, None] < length - 1) & ((length - 1 - steps)[:, None] < own_len[None, :])
    valid = jnp.stack([fore_valid, back_valid], axis=1).astype(jnp.float32)
    logit_sq = jnp.sum(valid[..., None] * logits * logits, axis=(0, 2, 3))
    top = jnp.max(logits, axis=-1, keepdims=True)
    log_total = top + jnp.log(jnp.sum(jnp.exp(logits - top), axis=-1, keepdims=True))
    target_hot = targets[..., None] == letters
    picked = jnp.sum(jnp.where(target_hot, logits, 0.0), axis=-1)
    loss = jnp.sum(valid * (log_total[..., 0] - picked))
    grad_logits = (
        valid[..., None] * (jnp.exp(logits - log_total) - target_hot.astype(jnp.float32)) / count
    ).astype(jnp.bfloat16)
    dec_bias = jnp.sum(grad_logits.astype(jnp.float32), axis=(0, 2))
    dec_grad = jnp.einsum("sdbh,sdbv->dhv", mine, grad_logits, preferred_element_type=jnp.float32)

    def backward_step(carry, inputs):
        grad_hidden, grad_cell = carry
        live, cell, in_gate, forget, cell_gate, out_gate, grad_logit = inputs
        grad_hidden = grad_hidden + jnp.einsum(
            "dbv,dhv->dbh", grad_logit, w_dec, preferred_element_type=jnp.float32
        )
        squash = jnp.tanh(forget * cell + in_gate * cell_gate)
        grad_new = jnp.where(
            live, grad_cell + grad_hidden * out_gate * (1.0 - squash * squash), 0.0
        )
        grad_out = jnp.where(live, grad_hidden * squash, 0.0)
        grad_pre = joined_gates(
            [
                grad_new * cell_gate * in_gate * (1.0 - in_gate),
                grad_new * cell * forget * (1.0 - forget),
                grad_new * in_gate * (1.0 - cell_gate * cell_gate),
                grad_out * out_gate * (1.0 - out_gate),
            ],
            lanes,
        ).astype(jnp.bfloat16)
        grad_cell_prev = grad_new * forget + jnp.where(live, 0.0, grad_cell)
        held = jnp.where(live, 0.0, grad_hidden)
        terms = jnp.einsum("dbc,dhc->dbh", grad_pre, w_rec, preferred_element_type=jnp.float32)
        through = lax.psum_scatter(
            terms.astype(jnp.bfloat16), "mp", scatter_dimension=2, tiled=True
        ).astype(jnp.float32)
        return ((held + through, grad_cell_prev), grad_pre)

    start = jnp.zeros(c_init.shape, jnp.float32)
    (hidden_grad, cell_grad), grad_pres = lax.scan(
        backward_step, (start, start), (live_steps, cells, *gates, grad_logits), reverse=True
    )
    rec_grad = jnp.einsum("sdbh,sdbc->dhc", wholes, grad_pres, preferred_element_type=jnp.float32)
    letter_grad = jnp.einsum(
        "sdbv,sdbc->dvc", onehot, grad_pres, preferred_element_type=jnp.float32
    )
    return (
        loss,
        hidden_sq,
        logit_sq,
        dec_bias,
        dec_grad,
        hidden_grad,
        cell_grad,
        rec_grad,
        letter_grad,
    )


def per_device(ids, lengths, order, h_init, c_init, embed, w_in, w_rec, bias, w_dec, b_dec):
    seq_rank = lax.axis_index("seq")
    first_mp = (lax.axis_index("mp") == 0).astype(jnp.float32)
    streams = ids.shape[1]
    per_dev = h_init.shape[1]
    own_units, all_units = (h_init.shape[2], w_rec.shape[1])
    letter_count = embed.shape[1]
    wd_full = lax.all_gather(w_dec, "mp", axis=1, tiled=True)
    whole_ids = lax.all_gather(ids, "seq", axis=0, tiled=True)
    own_order = lax.dynamic_slice_in_dim(order, seq_rank * per_dev, per_dev)
    slot_ids = jnp.take(whole_ids, own_order, axis=1)
    own_len = jnp.take(lengths, own_order)
    live_total = jnp.sum(lengths).astype(jnp.float32)
    count = 2.0 * (jnp.sum(lengths) - streams).astype(jnp.float32)
    step_ids = jnp.stack([slot_ids, jnp.flip(slot_ids, 0)])
    lanes, matrix = column_order(own_units)
    w_rec_grouped = grouped(w_rec, matrix)
    w_in_grouped = grouped(w_in, matrix)
    bias_grouped = jnp.swapaxes(bias.reshape(2, own_units // lanes, lanes, 4), -1, -2).reshape(
        bias.shape
    )
    loss, hidden_sq, logit_sq, dec_bias, dec_grad, hidden_grad, cell_grad, rec_grad, letter_grad = (
        recurrences(
            step_ids,
            own_len,
            h_init,
            c_init,
            embed,
            w_in_grouped,
            w_rec_grouped,
            bias_grouped,
            w_dec,
            wd_full,
            b_dec,
            count,
            lanes,
        )
    )
    embed_wide = embed.astype(jnp.float32)
    in_grad = jnp.einsum("dve,dvc->dec", embed_wide, letter_grad, precision=lax.Precision.HIGHEST)
    bias_grad = jnp.sum(letter_grad, axis=1, keepdims=True)
    embed_part = jnp.einsum(
        "dvc,dec->dve",
        letter_grad,
        w_in_grouped.astype(jnp.float32),
        precision=lax.Precision.HIGHEST,
    )
    edge = ungrouped_wide(jnp.concatenate([in_grad, bias_grad], axis=1), lanes)
    rec_part = lax.psum_scatter(
        rec_grad.astype(jnp.bfloat16), "seq", scatter_dimension=1, tiled=True
    )
    edge_part = lax.psum_scatter(edge.astype(jnp.bfloat16), "seq", scatter_dimension=2, tiled=True)
    dec_part = lax.psum_scatter(
        dec_grad.astype(jnp.bfloat16), "seq", scatter_dimension=1, tiled=True
    )
    loss_sum, hidden_all, logit_all, dec_bias_grad, embed_grad = lax.psum(
        (loss * first_mp, hidden_sq, logit_sq * first_mp, dec_bias * first_mp, embed_part),
        ("seq", "mp"),
    )
    rec_out = ungrouped(rec_part, matrix).astype(jnp.float32)
    rms_embed = jnp.sqrt(jnp.mean(embed_wide * embed_wide, axis=(1, 2)))
    return (
        loss_sum / count,
        hidden_grad,
        cell_grad,
        embed_grad,
        edge_part[:, :-1].astype(jnp.float32),
        rec_out,
        edge_part[:, -1].astype(jnp.float32),
        dec_part.astype(jnp.float32),
        dec_bias_grad,
        rms_embed,
        jnp.sqrt(hidden_all / (all_units * live_total)),
        jnp.sqrt(logit_all / (letter_count * count / 2.0)),
    )


def solution(mesh):
    in_specs = (
        P("seq", None),
        P(),
        P(),
        P(None, "seq", "mp"),
        P(None, "seq", "mp"),
        P(),
        P(None, None, "mp"),
        P(None, None, "mp"),
        P(None, "mp"),
        P(None, "mp", None),
        P(),
    )
    out_specs = (
        P(),
        P(None, "seq", "mp"),
        P(None, "seq", "mp"),
        P(),
        P(None, None, ("mp", "seq")),
        P(None, "seq", "mp"),
        P(None, ("mp", "seq")),
        P(None, ("mp", "seq"), None),
        P(),
        P(),
        P(),
        P(),
    )
    return jax.shard_map(
        per_device, mesh=mesh, in_specs=in_specs, out_specs=out_specs, check_vma=False
    )
```

profile of v0, /device:TPU:0, one launch (start us, length us, event | category | flops | bytes accessed | tf_op | source)
XLA Modules:
  0.0 2771.7 jit_solution(1599841801548186822)
XLA Ops:
  63.6 1312.1 %while.45 = (s32[]{:T(128)}, bf16[2,256,256]{2,1,0:T(8,128)(2,1)S(1)}, f32[2,256,256]{2,1,0:T(8,128)S(1)}, bf16[16,2,256,2048]{3,2,1,0:T(8,128)(2,1)}, f32[16,2,...) while((s32[]{:T(128)}, ...), condition=%wide.wide.region_1.2_spmd, body=%wide.wide.region_0.1_spmd.sunk | while | flops 2151284736 | bytes 70526840 | solution.py:80
  67.3 29.4 %all-gather.9.cloned.1.call-done = bf16[2,256,2048]{2,1,0:T(8,128)(2,1)} async-done(((bf16[2,256,256]{2,1,0:T(8,128)(2,1)}), bf16[2,256,2048]{2,1,0:T(8,128)(2,1)}) %all-gather.9.cloned.1.call-update) | async-done | bytes 2097168 | tf_op jit(solution)/shard_map/while/body/eval_jaxpr/all_gather | solution.py:67
  150.5 28.2 %all-gather.9.cloned.1.call-done = bf16[2,256,2048]{2,1,0:T(8,128)(2,1)} async-done(((bf16[2,256,256]{2,1,0:T(8,128)(2,1)}), bf16[2,256,2048]{2,1,0:T(8,128)(2,1)}) %all-gather.9.cloned.1.call-update) | async-done | bytes 2097168 | tf_op jit(solution)/shard_map/while/body/eval_jaxpr/all_gather | solution.py:67
  232.6 28.2 %all-gather.9.cloned.1.call-done = bf16[2,256,2048]{2,1,0:T(8,128)(2,1)} async-done(((bf16[2,256,256]{2,1,0:T(8,128)(2,1)}), bf16[2,256,2048]{2,1,0:T(8,128)(2,1)}) %all-gather.9.cloned.1.call-update) | async-done | bytes 2097168 | tf_op jit(solution)/shard_map/while/body/eval_jaxpr/all_gather | solution.py:67
  1470.3 954.1 %while.44 = (s32[]{:T(128)}, f32[2,256,256]{1,2,0:T(8,128)}, f32[2,256,256]{1,2,0:T(8,128)}, bf16[16,2,256,1024]{3,2,1,0:T(8,128)(2,1)}, pred[16,2,256,1]{2,1,3,...) while((s32[]{:T(128)}, f32[2,256,256]{1,2,0:T(8,128)}, ...), condition=%wide.region_10.11_spmd.clone, body=%wide.region_8.10_spmd.clone.sunk | while | flops 2227306496 | bytes 52475628 | solution.py:138
  1488.5 39.5 %reduce-scatter.11.cloned.1.call-done = bf16[2,256,256]{1,2,0:T(8,128)(2,1)} async-done(((bf16[2,256,2048]{1,2,0:T(8,128)(2,1)}), bf16[2,256,256]{1,2,0:T(8,128)(2,1)}) %reduce-scatter.11.cloned.1.call-update) | async-done | bytes 262160 | tf_op jit(solution)/shard_map/while/body/eval_jaxpr/reduce_scatter | solution.py:132
  1548.2 39.5 %reduce-scatter.11.cloned.1.call-done = bf16[2,256,256]{1,2,0:T(8,128)(2,1)} async-done(((bf16[2,256,2048]{1,2,0:T(8,128)(2,1)}), bf16[2,256,256]{1,2,0:T(8,128)(2,1)}) %reduce-scatter.11.cloned.1.call-update) | async-done | bytes 262160 | tf_op jit(solution)/shard_map/while/body/eval_jaxpr/reduce_scatter | solution.py:132
  1607.8 39.5 %reduce-scatter.11.cloned.1.call-done = bf16[2,256,256]{1,2,0:T(8,128)(2,1)} async-done(((bf16[2,256,2048]{1,2,0:T(8,128)(2,1)}), bf16[2,256,256]{1,2,0:T(8,128)(2,1)}) %reduce-scatter.11.cloned.1.call-update) | async-done | bytes 262160 | tf_op jit(solution)/shard_map/while/body/eval_jaxpr/reduce_scatter | solution.py:132
  1667.4 39.6 %reduce-scatter.11.cloned.1.call-done = bf16[2,256,256]{1,2,0:T(8,128)(2,1)} async-done(((bf16[2,256,2048]{1,2,0:T(8,128)(2,1)}), bf16[2,256,256]{1,2,0:T(8,128)(2,1)}) %reduce-scatter.11.cloned.1.call-update) | async-done | bytes 262160 | tf_op jit(solution)/shard_map/while/body/eval_jaxpr/reduce_scatter | solution.py:132
  1727.0 39.6 %reduce-scatter.11.cloned.1.call-done = bf16[2,256,256]{1,2,0:T(8,128)(2,1)} async-done(((bf16[2,256,2048]{1,2,0:T(8,128)(2,1)}), bf16[2,256,256]{1,2,0:T(8,128)(2,1)}) %reduce-scatter.11.cloned.1.call-update) | async-done | bytes 262160 | tf_op jit(solution)/shard_map/while/body/eval_jaxpr/reduce_scatter | solution.py:132
  1786.7 39.5 %reduce-scatter.11.cloned.1.call-done = bf16[2,256,256]{1,2,0:T(8,128)(2,1)} async-done(((bf16[2,256,2048]{1,2,0:T(8,128)(2,1)}), bf16[2,256,256]{1,2,0:T(8,128)(2,1)}) %reduce-scatter.11.cloned.1.call-update) | async-done | bytes 262160 | tf_op jit(solution)/shard_map/while/body/eval_jaxpr/reduce_scatter | solution.py:132
  1846.3 39.5 %reduce-scatter.11.cloned.1.call-done = bf16[2,256,256]{1,2,0:T(8,128)(2,1)} async-done(((bf16[2,256,2048]{1,2,0:T(8,128)(2,1)}), bf16[2,256,256]{1,2,0:T(8,128)(2,1)}) %reduce-scatter.11.cloned.1.call-update) | async-done | bytes 262160 | tf_op jit(solution)/shard_map/while/body/eval_jaxpr/reduce_scatter | solution.py:132
  1905.9 39.6 %reduce-scatter.11.cloned.1.call-done = bf16[2,256,256]{1,2,0:T(8,128)(2,1)} async-done(((bf16[2,256,2048]{1,2,0:T(8,128)(2,1)}), bf16[2,256,256]{1,2,0:T(8,128)(2,1)}) %reduce-scatter.11.cloned.1.call-update) | async-done | bytes 262160 | tf_op jit(solution)/shard_map/while/body/eval_jaxpr/reduce_scatter | solution.py:132
  1965.6 39.5 %reduce-scatter.11.cloned.1.call-done = bf16[2,256,256]{1,2,0:T(8,128)(2,1)} async-done(((bf16[2,256,2048]{1,2,0:T(8,128)(2,1)}), bf16[2,256,256]{1,2,0:T(8,128)(2,1)}) %reduce-scatter.11.cloned.1.call-update) | async-done | bytes 262160 | tf_op jit(solution)/shard_map/while/body/eval_jaxpr/reduce_scatter | solution.py:132
  2025.2 39.5 %reduce-scatter.11.cloned.1.call-done = bf16[2,256,256]{1,2,0:T(8,128)(2,1)} async-done(((bf16[2,256,2048]{1,2,0:T(8,128)(2,1)}), bf16[2,256,256]{1,2,0:T(8,128)(2,1)}) %reduce-scatter.11.cloned.1.call-update) | async-done | bytes 262160 | tf_op jit(solution)/shard_map/while/body/eval_jaxpr/reduce_scatter | solution.py:132
  2084.8 39.6 %reduce-scatter.11.cloned.1.call-done = bf16[2,256,256]{1,2,0:T(8,128)(2,1)} async-done(((bf16[2,256,2048]{1,2,0:T(8,128)(2,1)}), bf16[2,256,256]{1,2,0:T(8,128)(2,1)}) %reduce-scatter.11.cloned.1.call-update) | async-done | bytes 262160 | tf_op jit(solution)/shard_map/while/body/eval_jaxpr/reduce_scatter | solution.py:132
  2144.4 39.6 %reduce-scatter.11.cloned.1.call-done = bf16[2,256,256]{1,2,0:T(8,128)(2,1)} async-done(((bf16[2,256,2048]{1,2,0:T(8,128)(2,1)}), bf16[2,256,256]{1,2,0:T(8,128)(2,1)}) %reduce-scatter.11.cloned.1.call-update) | async-done | bytes 262160 | tf_op jit(solution)/shard_map/while/body/eval_jaxpr/reduce_scatter | solution.py:132
  2204.2 39.5 %reduce-scatter.11.cloned.1.call-done = bf16[2,256,256]{1,2,0:T(8,128)(2,1)} async-done(((bf16[2,256,2048]{1,2,0:T(8,128)(2,1)}), bf16[2,256,256]{1,2,0:T(8,128)(2,1)}) %reduce-scatter.11.cloned.1.call-update) | async-done | bytes 262160 | tf_op jit(solution)/shard_map/while/body/eval_jaxpr/reduce_scatter | solution.py:132
  2263.7 39.6 %reduce-scatter.11.cloned.1.call-done = bf16[2,256,256]{1,2,0:T(8,128)(2,1)} async-done(((bf16[2,256,2048]{1,2,0:T(8,128)(2,1)}), bf16[2,256,256]{1,2,0:T(8,128)(2,1)}) %reduce-scatter.11.cloned.1.call-update) | async-done | bytes 262160 | tf_op jit(solution)/shard_map/while/body/eval_jaxpr/reduce_scatter | solution.py:132
  2323.4 39.5 %reduce-scatter.11.cloned.1.call-done = bf16[2,256,256]{1,2,0:T(8,128)(2,1)} async-done(((bf16[2,256,2048]{1,2,0:T(8,128)(2,1)}), bf16[2,256,256]{1,2,0:T(8,128)(2,1)}) %reduce-scatter.11.cloned.1.call-update) | async-done | bytes 262160 | tf_op jit(solution)/shard_map/while/body/eval_jaxpr/reduce_scatter | solution.py:132
  2383.0 39.6 %reduce-scatter.11.cloned.1.call-done = bf16[2,256,256]{1,2,0:T(8,128)(2,1)} async-done(((bf16[2,256,2048]{1,2,0:T(8,128)(2,1)}), bf16[2,256,256]{1,2,0:T(8,128)(2,1)}) %reduce-scatter.11.cloned.1.call-update) | async-done | bytes 262160 | tf_op jit(solution)/shard_map/while/body/eval_jaxpr/reduce_scatter | solution.py:132
  2445.5 42.9 %bitcast_convert_fusion = bf16[2,2048,1024]{2,1,0:T(8,128)(2,1)} fusion(bf16[16,2,256,2048]{3,2,1,0:T(8,128)(2,1)} %get-tuple-element.342, bf16[16,2,256,1024]{3,2,1,0:T(8,128)(2,1)} %get-tuple-element.351), kind=kOutput, calls=%fused_computation.74 | convolution fusion | flops 34363932672 | bytes 58720256 | tf_op jit(solution)/shard_map/sdbh,sdbc->dhc/dot_general | solution.py:141
  2490.9 39.7 %all-reduce = (f32[]{:T(128)}, f32[2,275]{1,0:T(2,128)}, f32[2]{0:T(128)S(1)}, f32[2]{0:T(128)S(1)}) all-reduce(f32[]{:T(128)S(6)} %mul.239, f32[2,275]{1,0:T(2,128)S(1)} %broadcast_multiply_fusion, f32[2]{0:T(128)S(1)} %copy-done.23, f32[2]{0:T(128)S(1)} %broadcast_multiply_fusion.1), channel_id=1, replica_groups=mesh['seq'=4,'mp'=8] {'seq','mp'}, use_global_device_ids=true, to_apply=%region_6.7 | all-reduce | flops 555 | bytes 4440 | tf_op jit(solution)/shard_map/psum | solution.py:213
  2610.2 141.8 %reduce-scatter.7.cloned.1.call-done = bf16[2,512,1024]{2,1,0:T(8,128)(2,1)} async-done(((bf16[2,2048,1024]{2,1,0:T(8,128)(2,1)}), bf16[2,512,1024]{2,1,0:T(8,128)(2,1)}) %reduce-scatter.7.cloned.1.call-update) | async-done | bytes 2097168 | tf_op jit(solution)/shard_map/reduce_scatter | solution.py:206
  (999 shorter events, 1805.1 us)
Async XLA Ops:
  63.9 32.8 %all-gather.9.cloned.1.call-start = ((), (), s32[]{:S(2)}) async-start(), calls=%async_computation.11 | async-start | bytes 2359296 | tf_op jit(solution)/shard_map/while/body/eval_jaxpr/all_gather | solution.py:67
  638.5 31.7 %all-gather.9.cloned.1.call-start = ((), (), s32[]{:S(2)}) async-start(), calls=%async_computation.11 | async-start | bytes 2359296 | tf_op jit(solution)/shard_map/while/body/eval_jaxpr/all_gather | solution.py:67
  1375.7 50.2 %all-gather.5.cloned.1.call-start = ((), (), s32[]{:S(2)}) async-start(), calls=%async_computation.4 | async-start | bytes 2359296 | tf_op jit(solution)/shard_map/all_gather | solution.py:83
  1376.4 60.9 %all-gather.7.cloned.1.call-start = ((), (), s32[]{:S(2)}) async-start(), calls=%async_computation.5 | async-start | bytes 2580480 | tf_op jit(solution)/shard_map/all_gather | solution.py:165
  1470.5 57.6 %reduce-scatter.11.cloned.1.call-start = ((), (), s32[]{:S(2)}) async-start(), calls=%async_computation.10 | async-start | bytes 2359296 | tf_op jit(solution)/shard_map/while/body/eval_jaxpr/reduce_scatter | solution.py:132
  1529.8 57.8 %reduce-scatter.11.cloned.1.call-start = ((), (), s32[]{:S(2)}) async-start(), calls=%async_computation.10 | async-start | bytes 2359296 | tf_op jit(solution)/shard_map/while/body/eval_jaxpr/reduce_scatter | solution.py:132
  1589.5 57.8 %reduce-scatter.11.cloned.1.call-start = ((), (), s32[]{:S(2)}) async-start(), calls=%async_computation.10 | async-start | bytes 2359296 | tf_op jit(solution)/shard_map/while/body/eval_jaxpr/reduce_scatter | solution.py:132
  1649.1 57.8 %reduce-scatter.11.cloned.1.call-start = ((), (), s32[]{:S(2)}) async-start(), calls=%async_computation.10 | async-start | bytes 2359296 | tf_op jit(solution)/shard_map/while/body/eval_jaxpr/reduce_scatter | solution.py:132
  1708.7 57.8 %reduce-scatter.11.cloned.1.call-start = ((), (), s32[]{:S(2)}) async-start(), calls=%async_computation.10 | async-start | bytes 2359296 | tf_op jit(solution)/shard_map/while/body/eval_jaxpr/reduce_scatter | solution.py:132
  1768.4 57.8 %reduce-scatter.11.cloned.1.call-start = ((), (), s32[]{:S(2)}) async-start(), calls=%async_computation.10 | async-start | bytes 2359296 | tf_op jit(solution)/shard_map/while/body/eval_jaxpr/reduce_scatter | solution.py:132
  1828.0 57.8 %reduce-scatter.11.cloned.1.call-start = ((), (), s32[]{:S(2)}) async-start(), calls=%async_computation.10 | async-start | bytes 2359296 | tf_op jit(solution)/shard_map/while/body/eval_jaxpr/reduce_scatter | solution.py:132
  1887.6 57.8 %reduce-scatter.11.cloned.1.call-start = ((), (), s32[]{:S(2)}) async-start(), calls=%async_computation.10 | async-start | bytes 2359296 | tf_op jit(solution)/shard_map/while/body/eval_jaxpr/reduce_scatter | solution.py:132
  1947.3 57.8 %reduce-scatter.11.cloned.1.call-start = ((), (), s32[]{:S(2)}) async-start(), calls=%async_computation.10 | async-start | bytes 2359296 | tf_op jit(solution)/shard_map/while/body/eval_jaxpr/reduce_scatter | solution.py:132
  2006.9 57.8 %reduce-scatter.11.cloned.1.call-start = ((), (), s32[]{:S(2)}) async-start(), calls=%async_computation.10 | async-start | bytes 2359296 | tf_op jit(solution)/shard_map/while/body/eval_jaxpr/reduce_scatter | solution.py:132
  2066.5 57.8 %reduce-scatter.11.cloned.1.call-start = ((), (), s32[]{:S(2)}) async-start(), calls=%async_computation.10 | async-start | bytes 2359296 | tf_op jit(solution)/shard_map/while/body/eval_jaxpr/reduce_scatter | solution.py:132
  2126.2 57.9 %reduce-scatter.11.cloned.1.call-start = ((), (), s32[]{:S(2)}) async-start(), calls=%async_computation.10 | async-start | bytes 2359296 | tf_op jit(solution)/shard_map/while/body/eval_jaxpr/reduce_scatter | solution.py:132
  2185.8 57.8 %reduce-scatter.11.cloned.1.call-start = ((), (), s32[]{:S(2)}) async-start(), calls=%async_computation.10 | async-start | bytes 2359296 | tf_op jit(solution)/shard_map/while/body/eval_jaxpr/reduce_scatter | solution.py:132
  2245.4 57.9 %reduce-scatter.11.cloned.1.call-start = ((), (), s32[]{:S(2)}) async-start(), calls=%async_computation.10 | async-start | bytes 2359296 | tf_op jit(solution)/shard_map/while/body/eval_jaxpr/reduce_scatter | solution.py:132
  2305.1 57.8 %reduce-scatter.11.cloned.1.call-start = ((), (), s32[]{:S(2)}) async-start(), calls=%async_computation.10 | async-start | bytes 2359296 | tf_op jit(solution)/shard_map/while/body/eval_jaxpr/reduce_scatter | solution.py:132
  2364.7 57.9 %reduce-scatter.11.cloned.1.call-start = ((), (), s32[]{:S(2)}) async-start(), calls=%async_computation.10 | async-start | bytes 2359296 | tf_op jit(solution)/shard_map/while/body/eval_jaxpr/reduce_scatter | solution.py:132
  2424.4 135.9 %all-reduce.3.cloned.1.call-start = ((), (), s32[]{:S(2)}) async-start(), calls=%async_computation.6 | async-start | bytes 573440 | tf_op jit(solution)/shard_map/psum | solution.py:213
  2434.9 149.4 %reduce-scatter.9.cloned.1.call-start = ((), (), s32[]{:S(2)}) async-start(), calls=%async_computation.9 | async-start | bytes 491520 | tf_op jit(solution)/shard_map/reduce_scatter | solution.py:210
  2442.2 164.5 %reduce-scatter.5.cloned.1.call-start = ((), (), s32[]{:S(2)}) async-start(), calls=%async_computation.7 | async-start | bytes 655360 | tf_op jit(solution)/shard_map/reduce_scatter | solution.py:209
  2445.3 306.8 %reduce-scatter.7.cloned.1.call-start = ((), (), s32[]{:S(2)}) async-start(), calls=%async_computation.8 | async-start | bytes 10485760 | tf_op jit(solution)/shard_map/reduce_scatter | solution.py:206
  (116 other events, 5412.3 us)
Sparse Core Ops, SparseCore 0:
  67.3 29.3 all-gather.8
  150.6 28.1 all-gather.8
  232.6 28.1 all-gather.8
  396.1 28.1 all-gather.8
  559.9 28.1 all-gather.8
  641.9 28.1 all-gather.8
  723.9 28.1 all-gather.8
  805.7 28.1 all-gather.8
  1486.8 41.2 reduce-scatter.10
  1546.4 41.1 reduce-scatter.10
  1606.1 41.1 reduce-scatter.10
  1665.7 41.1 reduce-scatter.10
  1725.3 41.1 reduce-scatter.10
  1784.9 41.1 reduce-scatter.10
  1844.6 41.1 reduce-scatter.10
  1904.2 41.1 reduce-scatter.10
  1963.8 41.2 reduce-scatter.10
  2023.5 41.1 reduce-scatter.10
  2083.1 41.1 reduce-scatter.10
  2142.7 41.2 reduce-scatter.10
  2202.4 41.1 reduce-scatter.10
  2262.0 41.2 reduce-scatter.10
  2321.7 41.1 reduce-scatter.10
  2381.3 41.2 reduce-scatter.10
  (8 shorter events, 225.1 us)
Sparse Core Ops, SparseCore 1:
  1378.7 28.0 all-gather.4
  1408.4 28.9 all-gather.6
  2435.0 125.2 all-reduce.2
  2562.7 21.5 reduce-scatter.8
  2587.2 19.6 reduce-scatter.4
  2609.2 142.8 reduce-scatter.6
where the time goes:
time: 2790 us; the launch traced here: 2770 us
  waiting for transfers between devices  1300 us (47%)
  local copies, waits for them, and re-layouts  638 us (23%)
  other arithmetic  398 us (14%)
  matrix products  358 us (13%)
  blocking collectives  54.8 us (2%)
    reduce_scatter x16, waiting for transfers between devices, backward_step(): lax.psum_scatter(terms.astype(jnp.bfloat16), 'mp', scatter_dimension=2, t...  633 us
    all_gather x16, waiting for transfers between devices, forward_step(): whole = lax.all_gather(hidden, 'mp', axis=2, tiled=True)  450 us
    div x96, local copies, waits for them, and re-layouts, forward_step(): jax.nn.sigmoid(x)  173 us
    div x16, other arithmetic, forward_step(): jax.nn.sigmoid(x)  170 us
    reduce_scatter x1, waiting for transfers between devices, per_device(): lax.psum_scatter(rec_grad.astype(jnp.bfloat16), 'seq', scatter_dimension=...  142 us
    tanh x16, other arithmetic, forward_step(): cell_gate = jnp.tanh(cell_pre)  133 us
    dot_general x16, matrix products, backward_step(): jnp.einsum('dbc,dhc->dbh', grad_pre, w_rec, preferred_element_type=jnp.fl...  113 us
    dynamic_update_slice x64, local copies, waits for them, and re-layouts, recurrences(): lax.scan(forward_step, (h_init, c_init), (gates_in, live_steps))  110 us
  transfers between devices with their start and end apart: 38, of which 37 were waited for; matrix products, arithmetic and copies ran while one was open for 7% of the time, Pallas kernels for 0%

commit v1 on v0

--- a/solution.py
+++ b/solution.py
@@ -210,9 +210,13 @@
     dec_part = lax.psum_scatter(
         dec_grad.astype(jnp.bfloat16), "seq", scatter_dimension=1, tiled=True
     )
-    loss_sum, hidden_all, logit_all, dec_bias_grad, embed_grad = lax.psum(
-        (loss * first_mp, hidden_sq, logit_sq * first_mp, dec_bias * first_mp, embed_part),
-        ("seq", "mp"),
+
+    def finish_node(chunk):
+        high = jax.lax.psum(chunk, axis_name="seq")
+        return jax.lax.psum(high, "mp")
+
+    loss_sum, hidden_all, logit_all, dec_bias_grad, embed_grad = finish_node(
+        (loss * first_mp, hidden_sq, logit_sq * first_mp, dec_bias * first_mp, embed_part)
     )
     rec_out = ungrouped(rec_part, matrix).astype(jnp.float32)
     rms_embed = jnp.sqrt(jnp.mean(embed_wide * embed_wide, axis=(1, 2)))

time: 2790 us -> 2750 us (0.986)
  transfers between devices with their start and end apart: 38 -> 39, of which waited for: 37 -> 36; matrix products, arithmetic and copies ran while one was open for 7% -> 7% of each run, Pallas kernels for 0% -> 0%
where the time goes in v1:
time: 2750 us; the launch traced here: 2740 us
  waiting for transfers between devices  1280 us (47%)
  local copies, waits for them, and re-layouts  638 us (23%)
  other arithmetic  397 us (14%)
  matrix products  359 us (13%)
  blocking collectives  39.9 us (1%)
    reduce_scatter x16, waiting for transfers between devices, backward_step(): lax.psum_scatter(terms.astype(jnp.bfloat16), 'mp', scatter_dimension=2, t...  633 us
    all_gather x16, waiting for transfers between devices, forward_step(): whole = lax.all_gather(hidden, 'mp', axis=2, tiled=True)  448 us
    div x96, local copies, waits for them, and re-layouts, forward_step(): jax.nn.sigmoid(x)  173 us
    div x16, other arithmetic, forward_step(): jax.nn.sigmoid(x)  170 us
    reduce_scatter x1, waiting for transfers between devices, per_device(): lax.psum_scatter(rec_grad.astype(jnp.bfloat16), 'seq', scatter_dimension=...  142 us
    tanh x16, other arithmetic, forward_step(): cell_gate = jnp.tanh(cell_pre)  133 us
    dot_general x16, matrix products, backward_step(): jnp.einsum('dbc,dhc->dbh', grad_pre, w_rec, preferred_element_type=jnp.fl...  113 us
    dynamic_update_slice x64, local copies, waits for them, and re-layouts, recurrences(): lax.scan(forward_step, (h_init, c_init), (gates_in, live_steps))  109 us
  transfers between devices with their start and end apart: 39, of which 36 were waited for; matrix products, arithmetic and copies ran while one was open for 7% of the time, Pallas kernels for 0%

profile of v1, /device:TPU:0, one launch (start us, length us, event | category | flops | bytes accessed | tf_op | source)
XLA Modules:
  0.0 2736.5 jit_solution(15774350132596363155)
XLA Ops:
  64.2 1309.4 %while.45 = (s32[]{:T(128)}, bf16[2,256,256]{2,1,0:T(8,128)(2,1)S(1)}, f32[2,256,256]{2,1,0:T(8,128)S(1)}, bf16[16,2,256,2048]{3,2,1,0:T(8,128)(2,1)}, f32[16,2,...) while((s32[]{:T(128)}, ...), condition=%wide.wide.region_1.2_spmd, body=%wide.wide.region_0.1_spmd.sunk | while | flops 2151284736 | bytes 70526840 | solution.py:80
  67.9 29.2 %all-gather.9.cloned.1.call-done = bf16[2,256,2048]{2,1,0:T(8,128)(2,1)} async-done(((bf16[2,256,256]{2,1,0:T(8,128)(2,1)}), bf16[2,256,2048]{2,1,0:T(8,128)(2,1)}) %all-gather.9.cloned.1.call-update) | async-done | bytes 2097168 | tf_op jit(solution)/shard_map/while/body/eval_jaxpr/all_gather | solution.py:67
  151.0 28.1 %all-gather.9.cloned.1.call-done = bf16[2,256,2048]{2,1,0:T(8,128)(2,1)} async-done(((bf16[2,256,256]{2,1,0:T(8,128)(2,1)}), bf16[2,256,2048]{2,1,0:T(8,128)(2,1)}) %all-gather.9.cloned.1.call-update) | async-done | bytes 2097168 | tf_op jit(solution)/shard_map/while/body/eval_jaxpr/all_gather | solution.py:67
  232.8 28.1 %all-gather.9.cloned.1.call-done = bf16[2,256,2048]{2,1,0:T(8,128)(2,1)} async-done(((bf16[2,256,256]{2,1,0:T(8,128)(2,1)}), bf16[2,256,2048]{2,1,0:T(8,128)(2,1)}) %all-gather.9.cloned.1.call-update) | async-done | bytes 2097168 | tf_op jit(solution)/shard_map/while/body/eval_jaxpr/all_gather | solution.py:67
  1469.3 955.0 %while.44 = (s32[]{:T(128)}, f32[2,256,256]{1,2,0:T(8,128)}, f32[2,256,256]{1,2,0:T(8,128)}, bf16[16,2,256,1024]{3,2,1,0:T(8,128)(2,1)}, pred[16,2,256,1]{2,1,3,...) while((s32[]{:T(128)}, f32[2,256,256]{1,2,0:T(8,128)}, ...), condition=%wide.region_11.12_spmd.clone, body=%wide.region_9.11_spmd.clone.sunk | while | flops 2227306496 | bytes 52475628 | solution.py:138
  1487.5 39.6 %reduce-scatter.11.cloned.1.call-done = bf16[2,256,256]{1,2,0:T(8,128)(2,1)} async-done(((bf16[2,256,2048]{1,2,0:T(8,128)(2,1)}), bf16[2,256,256]{1,2,0:T(8,128)(2,1)}) %reduce-scatter.11.cloned.1.call-update) | async-done | bytes 262160 | tf_op jit(solution)/shard_map/while/body/eval_jaxpr/reduce_scatter | solution.py:132
  1547.2 39.5 %reduce-scatter.11.cloned.1.call-done = bf16[2,256,256]{1,2,0:T(8,128)(2,1)} async-done(((bf16[2,256,2048]{1,2,0:T(8,128)(2,1)}), bf16[2,256,256]{1,2,0:T(8,128)(2,1)}) %reduce-scatter.11.cloned.1.call-update) | async-done | bytes 262160 | tf_op jit(solution)/shard_map/while/body/eval_jaxpr/reduce_scatter | solution.py:132
  1606.9 39.6 %reduce-scatter.11.cloned.1.call-done = bf16[2,256,256]{1,2,0:T(8,128)(2,1)} async-done(((bf16[2,256,2048]{1,2,0:T(8,128)(2,1)}), bf16[2,256,256]{1,2,0:T(8,128)(2,1)}) %reduce-scatter.11.cloned.1.call-update) | async-done | bytes 262160 | tf_op jit(solution)/shard_map/while/body/eval_jaxpr/reduce_scatter | solution.py:132
  1666.6 39.6 %reduce-scatter.11.cloned.1.call-done = bf16[2,256,256]{1,2,0:T(8,128)(2,1)} async-done(((bf16[2,256,2048]{1,2,0:T(8,128)(2,1)}), bf16[2,256,256]{1,2,0:T(8,128)(2,1)}) %reduce-scatter.11.cloned.1.call-update) | async-done | bytes 262160 | tf_op jit(solution)/shard_map/while/body/eval_jaxpr/reduce_scatter | solution.py:132
  1726.2 39.6 %reduce-scatter.11.cloned.1.call-done = bf16[2,256,256]{1,2,0:T(8,128)(2,1)} async-done(((bf16[2,256,2048]{1,2,0:T(8,128)(2,1)}), bf16[2,256,256]{1,2,0:T(8,128)(2,1)}) %reduce-scatter.11.cloned.1.call-update) | async-done | bytes 262160 | tf_op jit(solution)/shard_map/while/body/eval_jaxpr/reduce_scatter | solution.py:132
  1785.9 39.6 %reduce-scatter.11.cloned.1.call-done = bf16[2,256,256]{1,2,0:T(8,128)(2,1)} async-done(((bf16[2,256,2048]{1,2,0:T(8,128)(2,1)}), bf16[2,256,256]{1,2,0:T(8,128)(2,1)}) %reduce-scatter.11.cloned.1.call-update) | async-done | bytes 262160 | tf_op jit(solution)/shard_map/while/body/eval_jaxpr/reduce_scatter | solution.py:132
  1845.7 39.5 %reduce-scatter.11.cloned.1.call-done = bf16[2,256,256]{1,2,0:T(8,128)(2,1)} async-done(((bf16[2,256,2048]{1,2,0:T(8,128)(2,1)}), bf16[2,256,256]{1,2,0:T(8,128)(2,1)}) %reduce-scatter.11.cloned.1.call-update) | async-done | bytes 262160 | tf_op jit(solution)/shard_map/while/body/eval_jaxpr/reduce_scatter | solution.py:132
  1905.3 39.6 %reduce-scatter.11.cloned.1.call-done = bf16[2,256,256]{1,2,0:T(8,128)(2,1)} async-done(((bf16[2,256,2048]{1,2,0:T(8,128)(2,1)}), bf16[2,256,256]{1,2,0:T(8,128)(2,1)}) %reduce-scatter.11.cloned.1.call-update) | async-done | bytes 262160 | tf_op jit(solution)/shard_map/while/body/eval_jaxpr/reduce_scatter | solution.py:132
  1965.0 39.6 %reduce-scatter.11.cloned.1.call-done = bf16[2,256,256]{1,2,0:T(8,128)(2,1)} async-done(((bf16[2,256,2048]{1,2,0:T(8,128)(2,1)}), bf16[2,256,256]{1,2,0:T(8,128)(2,1)}) %reduce-scatter.11.cloned.1.call-update) | async-done | bytes 262160 | tf_op jit(solution)/shard_map/while/body/eval_jaxpr/reduce_scatter | solution.py:132
  2024.7 39.6 %reduce-scatter.11.cloned.1.call-done = bf16[2,256,256]{1,2,0:T(8,128)(2,1)} async-done(((bf16[2,256,2048]{1,2,0:T(8,128)(2,1)}), bf16[2,256,256]{1,2,0:T(8,128)(2,1)}) %reduce-scatter.11.cloned.1.call-update) | async-done | bytes 262160 | tf_op jit(solution)/shard_map/while/body/eval_jaxpr/reduce_scatter | solution.py:132
  2084.4 39.6 %reduce-scatter.11.cloned.1.call-done = bf16[2,256,256]{1,2,0:T(8,128)(2,1)} async-done(((bf16[2,256,2048]{1,2,0:T(8,128)(2,1)}), bf16[2,256,256]{1,2,0:T(8,128)(2,1)}) %reduce-scatter.11.cloned.1.call-update) | async-done | bytes 262160 | tf_op jit(solution)/shard_map/while/body/eval_jaxpr/reduce_scatter | solution.py:132
  2144.1 39.6 %reduce-scatter.11.cloned.1.call-done = bf16[2,256,256]{1,2,0:T(8,128)(2,1)} async-done(((bf16[2,256,2048]{1,2,0:T(8,128)(2,1)}), bf16[2,256,256]{1,2,0:T(8,128)(2,1)}) %reduce-scatter.11.cloned.1.call-update) | async-done | bytes 262160 | tf_op jit(solution)/shard_map/while/body/eval_jaxpr/reduce_scatter | solution.py:132
  2203.8 39.5 %reduce-scatter.11.cloned.1.call-done = bf16[2,256,256]{1,2,0:T(8,128)(2,1)} async-done(((bf16[2,256,2048]{1,2,0:T(8,128)(2,1)}), bf16[2,256,256]{1,2,0:T(8,128)(2,1)}) %reduce-scatter.11.cloned.1.call-update) | async-done | bytes 262160 | tf_op jit(solution)/shard_map/while/body/eval_jaxpr/reduce_scatter | solution.py:132
  2263.5 39.6 %reduce-scatter.11.cloned.1.call-done = bf16[2,256,256]{1,2,0:T(8,128)(2,1)} async-done(((bf16[2,256,2048]{1,2,0:T(8,128)(2,1)}), bf16[2,256,256]{1,2,0:T(8,128)(2,1)}) %reduce-scatter.11.cloned.1.call-update) | async-done | bytes 262160 | tf_op jit(solution)/shard_map/while/body/eval_jaxpr/reduce_scatter | solution.py:132
  2323.2 39.5 %reduce-scatter.11.cloned.1.call-done = bf16[2,256,256]{1,2,0:T(8,128)(2,1)} async-done(((bf16[2,256,2048]{1,2,0:T(8,128)(2,1)}), bf16[2,256,256]{1,2,0:T(8,128)(2,1)}) %reduce-scatter.11.cloned.1.call-update) | async-done | bytes 262160 | tf_op jit(solution)/shard_map/while/body/eval_jaxpr/reduce_scatter | solution.py:132
  2382.9 39.6 %reduce-scatter.11.cloned.1.call-done = bf16[2,256,256]{1,2,0:T(8,128)(2,1)} async-done(((bf16[2,256,2048]{1,2,0:T(8,128)(2,1)}), bf16[2,256,256]{1,2,0:T(8,128)(2,1)}) %reduce-scatter.11.cloned.1.call-update) | async-done | bytes 262160 | tf_op jit(solution)/shard_map/while/body/eval_jaxpr/reduce_scatter | solution.py:132
  2441.0 29.4 %all-reduce.5.cloned.1.call-done = f32[2,275,100]{2,1,0:T(8,128)} async-done(((f32[2,275,100]{2,1,0:T(8,128)}), f32[2,275,100]{2,1,0:T(8,128)}) %all-reduce.5.cloned.1.call-update) | async-done | bytes 220016 | tf_op jit(solution)/shard_map/psum | solution.py:215
  2481.1 42.9 %bitcast_convert_fusion = bf16[2,2048,1024]{2,1,0:T(8,128)(2,1)} fusion(bf16[16,2,256,2048]{3,2,1,0:T(8,128)(2,1)} %get-tuple-element.342, bf16[16,2,256,1024]{3,2,1,0:T(8,128)(2,1)} %get-tuple-element.351), kind=kOutput, calls=%fused_computation.74 | convolution fusion | flops 34363932672 | bytes 58720256 | tf_op jit(solution)/shard_map/sdbh,sdbc->dhc/dot_general | solution.py:141
  2575.0 141.9 %reduce-scatter.7.cloned.1.call-done = bf16[2,512,1024]{2,1,0:T(8,128)(2,1)} async-done(((bf16[2,2048,1024]{2,1,0:T(8,128)(2,1)}), bf16[2,512,1024]{2,1,0:T(8,128)(2,1)}) %reduce-scatter.7.cloned.1.call-update) | async-done | bytes 2097168 | tf_op jit(solution)/shard_map/reduce_scatter | solution.py:206
  (1001 shorter events, 1780.3 us)
Async XLA Ops:
  64.5 32.6 %all-gather.9.cloned.1.call-start = ((), (), s32[]{:S(2)}) async-start(), calls=%async_computation.12 | async-start | bytes 2359296 | tf_op jit(solution)/shard_map/while/body/eval_jaxpr/all_gather | solution.py:67
  1373.7 50.2 %all-gather.5.cloned.1.call-start = ((), (), s32[]{:S(2)}) async-start(), calls=%async_computation.4 | async-start | bytes 2359296 | tf_op jit(solution)/shard_map/all_gather | solution.py:83
  1374.4 61.5 %all-gather.7.cloned.1.call-start = ((), (), s32[]{:S(2)}) async-start(), calls=%async_computation.5 | async-start | bytes 2580480 | tf_op jit(solution)/shard_map/all_gather | solution.py:165
  1469.4 57.6 %reduce-scatter.11.cloned.1.call-start = ((), (), s32[]{:S(2)}) async-start(), calls=%async_computation.11 | async-start | bytes 2359296 | tf_op jit(solution)/shard_map/while/body/eval_jaxpr/reduce_scatter | solution.py:132
  1528.9 57.9 %reduce-scatter.11.cloned.1.call-start = ((), (), s32[]{:S(2)}) async-start(), calls=%async_computation.11 | async-start | bytes 2359296 | tf_op jit(solution)/shard_map/while/body/eval_jaxpr/reduce_scatter | solution.py:132
  1588.6 57.9 %reduce-scatter.11.cloned.1.call-start = ((), (), s32[]{:S(2)}) async-start(), calls=%async_computation.11 | async-start | bytes 2359296 | tf_op jit(solution)/shard_map/while/body/eval_jaxpr/reduce_scatter | solution.py:132
  1648.3 57.9 %reduce-scatter.11.cloned.1.call-start = ((), (), s32[]{:S(2)}) async-start(), calls=%async_computation.11 | async-start | bytes 2359296 | tf_op jit(solution)/shard_map/while/body/eval_jaxpr/reduce_scatter | solution.py:132
  1707.9 57.9 %reduce-scatter.11.cloned.1.call-start = ((), (), s32[]{:S(2)}) async-start(), calls=%async_computation.11 | async-start | bytes 2359296 | tf_op jit(solution)/shard_map/while/body/eval_jaxpr/reduce_scatter | solution.py:132
  1767.6 57.9 %reduce-scatter.11.cloned.1.call-start = ((), (), s32[]{:S(2)}) async-start(), calls=%async_computation.11 | async-start | bytes 2359296 | tf_op jit(solution)/shard_map/while/body/eval_jaxpr/reduce_scatter | solution.py:132
  1827.3 57.9 %reduce-scatter.11.cloned.1.call-start = ((), (), s32[]{:S(2)}) async-start(), calls=%async_computation.11 | async-start | bytes 2359296 | tf_op jit(solution)/shard_map/while/body/eval_jaxpr/reduce_scatter | solution.py:132
  1887.0 57.9 %reduce-scatter.11.cloned.1.call-start = ((), (), s32[]{:S(2)}) async-start(), calls=%async_computation.11 | async-start | bytes 2359296 | tf_op jit(solution)/shard_map/while/body/eval_jaxpr/reduce_scatter | solution.py:132
  1946.7 57.9 %reduce-scatter.11.cloned.1.call-start = ((), (), s32[]{:S(2)}) async-start(), calls=%async_computation.11 | async-start | bytes 2359296 | tf_op jit(solution)/shard_map/while/body/eval_jaxpr/reduce_scatter | solution.py:132
  2006.4 57.9 %reduce-scatter.11.cloned.1.call-start = ((), (), s32[]{:S(2)}) async-start(), calls=%async_computation.11 | async-start | bytes 2359296 | tf_op jit(solution)/shard_map/while/body/eval_jaxpr/reduce_scatter | solution.py:132
  2066.1 57.9 %reduce-scatter.11.cloned.1.call-start = ((), (), s32[]{:S(2)}) async-start(), calls=%async_computation.11 | async-start | bytes 2359296 | tf_op jit(solution)/shard_map/while/body/eval_jaxpr/reduce_scatter | solution.py:132
  2125.8 57.9 %reduce-scatter.11.cloned.1.call-start = ((), (), s32[]{:S(2)}) async-start(), calls=%async_computation.11 | async-start | bytes 2359296 | tf_op jit(solution)/shard_map/while/body/eval_jaxpr/reduce_scatter | solution.py:132
  2185.5 57.9 %reduce-scatter.11.cloned.1.call-start = ((), (), s32[]{:S(2)}) async-start(), calls=%async_computation.11 | async-start | bytes 2359296 | tf_op jit(solution)/shard_map/while/body/eval_jaxpr/reduce_scatter | solution.py:132
  2245.2 57.9 %reduce-scatter.11.cloned.1.call-start = ((), (), s32[]{:S(2)}) async-start(), calls=%async_computation.11 | async-start | bytes 2359296 | tf_op jit(solution)/shard_map/while/body/eval_jaxpr/reduce_scatter | solution.py:132
  2304.8 57.9 %reduce-scatter.11.cloned.1.call-start = ((), (), s32[]{:S(2)}) async-start(), calls=%async_computation.11 | async-start | bytes 2359296 | tf_op jit(solution)/shard_map/while/body/eval_jaxpr/reduce_scatter | solution.py:132
  2364.6 57.9 %reduce-scatter.11.cloned.1.call-start = ((), (), s32[]{:S(2)}) async-start(), calls=%async_computation.11 | async-start | bytes 2359296 | tf_op jit(solution)/shard_map/while/body/eval_jaxpr/reduce_scatter | solution.py:132
  2424.3 46.1 %all-reduce.5.cloned.1.call-start = ((), (), s32[]{:S(2)}) async-start(), calls=%async_computation.6 | async-start | bytes 573440 | tf_op jit(solution)/shard_map/psum | solution.py:215
  2434.8 120.1 %all-reduce.7.cloned.1.call-start = ((), (), s32[]{:S(2)}) async-start(), calls=%async_computation.7 | async-start | bytes 573440 | tf_op jit(solution)/shard_map/psum | solution.py:216
  2470.4 86.4 %reduce-scatter.9.cloned.1.call-start = ((), (), s32[]{:S(2)}) async-start(), calls=%async_computation.10 | async-start | bytes 491520 | tf_op jit(solution)/shard_map/reduce_scatter | solution.py:210
  2478.0 93.6 %reduce-scatter.5.cloned.1.call-start = ((), (), s32[]{:S(2)}) async-start(), calls=%async_computation.8 | async-start | bytes 655360 | tf_op jit(solution)/shard_map/reduce_scatter | solution.py:209
  2481.0 235.9 %reduce-scatter.7.cloned.1.call-start = ((), (), s32[]{:S(2)}) async-start(), calls=%async_computation.9 | async-start | bytes 10485760 | tf_op jit(solution)/shard_map/reduce_scatter | solution.py:206
  (116 other events, 5385.0 us)
Sparse Core Ops, SparseCore 0:
  67.8 29.3 all-gather.8
  314.2 28.1 all-gather.8
  477.4 28.1 all-gather.8
  886.5 28.1 all-gather.8
  968.0 28.1 all-gather.8
  1131.5 28.1 all-gather.8
  1213.1 28.1 all-gather.8
  1294.6 28.1 all-gather.8
  1485.8 41.2 reduce-scatter.10
  1545.5 41.2 reduce-scatter.10
  1605.2 41.2 reduce-scatter.10
  1664.9 41.2 reduce-scatter.10
  1724.6 41.2 reduce-scatter.10
  1784.2 41.2 reduce-scatter.10
  1843.9 41.2 reduce-scatter.10
  1903.6 41.2 reduce-scatter.10
  1963.3 41.2 reduce-scatter.10
  2023.0 41.2 reduce-scatter.10
  2082.7 41.2 reduce-scatter.10
  2142.4 41.2 reduce-scatter.10
  2202.1 41.2 reduce-scatter.10
  2261.8 41.2 reduce-scatter.10
  2321.5 41.2 reduce-scatter.10
  2381.2 41.2 reduce-scatter.10
  (8 shorter events, 225.1 us)
Sparse Core Ops, SparseCore 1:
  1376.6 28.0 all-gather.4
  1406.9 28.9 all-gather.6
  2434.9 35.4 all-reduce.4
  2473.5 51.8 all-reduce.6
  2527.7 21.2 reduce-scatter.8
  2551.9 19.6 reduce-scatter.4
  2573.9 142.9 reduce-scatter.6
